TPU v7x, 32 devices: a whole 2x2x4 slice. The times are simulated.
32 devices in a mesh: tp: 8 (over y, x, core), dp: 4 (over z).
Axes of the slice: x: 2, y: 2, z: 4, core: 2. Of those that a mesh axis runs over, the one named last changes fastest.
Arguments:
- activations: bfloat16 [64, 512, 4096], P('dp', None, 'tp'), may hold values from -6 to 6
- query_output_cotangent: bfloat16 [64, 512, 4096], P('dp', None, 'tp'), may hold values from -6 to 6
- value_output_cotangent: bfloat16 [64, 512, 4096], P('dp', None, 'tp'), may hold values from -6 to 6
- lengths: int32 [64], P('dp'), may hold values from 1 to 512
- reducing_matrices_pair: bfloat16 [2, 4096, 128], P(None, 'tp'), may hold values from -0.09375 to 0.09375
- expanding_matrices_pair: bfloat16 [2, 128, 4096], P(None, None, 'tp'), may hold values from -0.5 to 0.5
- width_side_projections: bfloat16 [2, 4096, 128], P(None, 'tp'), may hold values from -0.09375 to 0.09375
- narrow_random_sketch: bfloat16 [128, 16], replicated, may hold values from -0.5 to 0.5
- projected_first_moment: float32 [8192], replicated, may hold values from -6 to 6
- projected_second_moment: float32 [8192], replicated, may hold values from 0.1 to 10
- targets: bfloat16 [1024, 8192], P('dp', 'tp'), may hold values from -6 to 6
Outputs:
- scores: float32 [64, 1024], P('dp', 'tp')
All inputs are finite; a program needn't handle non-finite values.
Results may differ from a plain program's by a relative error of at most 0.023.
Values may be sent and summed in bfloat16 or wider, within the bound.
A program may use at most 128 MiB of HBM per device.

v0:
```python
import math
import jax
import jax.numpy as jnp
from jax import lax
from jax.sharding import PartitionSpec as P


def adam_update(features, first_moment, second_moment):
    mixed = 0.9 * first_moment + 0.1 * features
    spread = 0.999 * second_moment + 0.001 * features * features
    return mixed / (jnp.sqrt(spread) + 1e-08)


def combine_factors(reducing_matrices_pair, expanding_matrices_pair, narrow_random_sketch):
    attention_key_reducer = jnp.dot(
        reducing_matrices_pair[0], narrow_random_sketch, preferred_element_type=jnp.float32
    ).astype(jnp.bfloat16)
    value_down_factor = jnp.dot(
        reducing_matrices_pair[1], narrow_random_sketch, preferred_element_type=jnp.float32
    ).astype(jnp.bfloat16)
    query_up_factor = jnp.dot(
        expanding_matrices_pair[0].T, narrow_random_sketch, preferred_element_type=jnp.float32
    ).astype(jnp.bfloat16)
    value_up_factor = jnp.dot(
        expanding_matrices_pair[1].T, narrow_random_sketch, preferred_element_type=jnp.float32
    ).astype(jnp.bfloat16)
    return (attention_key_reducer, value_down_factor, query_up_factor, value_up_factor)


def body(
    activations,
    query_output_cotangent,
    value_output_cotangent,
    lengths,
    reducing_matrices_pair,
    expanding_matrices_pair,
    width_side_projections,
    narrow_random_sketch,
    projected_first_moment,
    projected_second_moment,
    targets,
):
    attention_key_reducer, value_down_factor, query_up_factor, value_up_factor = combine_factors(
        reducing_matrices_pair, expanding_matrices_pair, narrow_random_sketch
    )
    rank_cols = narrow_random_sketch.shape[1]
    w_left = jnp.concatenate(
        [attention_key_reducer, value_down_factor, width_side_projections[0]], axis=1
    )
    w_query = jnp.concatenate([query_up_factor, width_side_projections[1]], axis=1)
    w_value = jnp.concatenate([value_up_factor, width_side_projections[1]], axis=1)
    groups = lax.axis_size("tp")
    parts = lax.axis_size("dp")
    member = lax.axis_index("tp")
    local_ex, seq_len = activations.shape[:2]
    feature_count = projected_first_moment.shape[0]
    positions = jnp.arange(seq_len, dtype=jnp.int32)
    token_mask = (positions[None, :] < lengths[:, None])[..., None]

    def project(rows, weights):
        out = jnp.einsum("esd,dc->esc", rows, weights, preferred_element_type=jnp.float32)
        return out.astype(jnp.bfloat16)

    left = project(activations, w_left)
    right_q = project(query_output_cotangent, w_query)
    right_v = project(value_output_cotangent, w_value)
    narrow = jnp.concatenate(
        [left[..., : 2 * rank_cols], right_q[..., :rank_cols], right_v[..., :rank_cols]], axis=-1
    )
    narrow = jnp.where(token_mask, narrow, jnp.zeros((), jnp.bfloat16))
    narrow = lax.psum(narrow, "tp")

    def outer_sum(first, wide):
        return jnp.einsum(
            "esr,esk->erk",
            narrow[..., first * rank_cols : (first + 1) * rank_cols],
            wide,
            preferred_element_type=jnp.float32,
        )

    own_features = jnp.concatenate(
        [
            outer_sum(2, left[..., 2 * rank_cols :]),
            outer_sum(3, left[..., 2 * rank_cols :]),
            outer_sum(0, right_q[..., rank_cols:]),
            outer_sum(1, right_v[..., rank_cols:]),
        ],
        axis=1,
    ).reshape(local_ex, -1)
    features = lax.psum_scatter(
        own_features.astype(jnp.bfloat16), "tp", scatter_dimension=1, tiled=True
    ).astype(jnp.float32)
    span = feature_count // groups
    first_moment = lax.dynamic_slice_in_dim(projected_first_moment, member * span, span)
    second_moment = lax.dynamic_slice_in_dim(projected_second_moment, member * span, span)
    update = adam_update(features, first_moment, second_moment).astype(jnp.bfloat16)
    update = lax.all_gather(update, "dp", axis=0, tiled=True)
    wide_update = update.astype(jnp.float32)
    target_float = targets.astype(jnp.float32)
    update_sq = jnp.sum(wide_update * wide_update, axis=1)
    target_sq = jnp.sum(target_float * target_float, axis=1)
    dots = lax.dot_general(
        update, targets, (((1,), (1,)), ((), ())), preferred_element_type=jnp.float32
    )
    rows = jnp.concatenate(
        [dots, jnp.broadcast_to(update_sq[:, None], (dots.shape[0], 128))], axis=1
    ).reshape(parts, local_ex, -1)
    extra = jnp.pad(target_sq, (0, 128))
    rows = jnp.concatenate([rows, jnp.broadcast_to(extra, (parts, 8, extra.shape[0]))], axis=1)
    rows = lax.psum(rows, "tp")
    rows = lax.all_to_all(rows, "dp", split_axis=0, concat_axis=0, tiled=True)
    owned = targets.shape[0]
    totals = jnp.moveaxis(rows[:, :, :owned], 0, 1).reshape(local_ex + 8, parts * owned)
    columns = parts * owned // groups
    totals = lax.dynamic_slice_in_dim(totals, member * columns, columns, 1)
    row_scale = lax.rsqrt(rows[0, :local_ex, owned : owned + 1] + 1e-06)
    column_scale = lax.rsqrt(totals[local_ex : local_ex + 1] + 1e-06)
    return totals[:local_ex] * row_scale * column_scale * math.sqrt(feature_count)


def solution(mesh):
    placed = (
        P("dp", None, "tp"),
        P("dp", None, "tp"),
        P("dp", None, "tp"),
        P("dp"),
        P(None, "tp", None),
        P(None, None, "tp"),
        P(None, "tp", None),
        P(),
        P(),
        P(),
        P("dp", "tp"),
    )
    return jax.shard_map(body, mesh=mesh, in_specs=placed, out_specs=P("dp", "tp"), check_vma=False)
```

profile of v0, /device:TPU:0, one launch (start us, length us, event | category | flops | bytes accessed | tf_op | source)
XLA Modules:
  0.0 220.2 jit_solution(16352123582546980845)
XLA Ops:
  6.5 0.0 copy-start
  6.5 0.0 all-reduce.4.cloned.1.call-start
  6.5 0.7 copy-done
  7.2 1.0 convolution_convert_fusion.2
  8.3 1.1 convolution_convert_fusion.3
  9.3 1.0 convolution_convert_fusion.1
  10.4 1.0 convolution_convert_fusion
  11.4 1.0 fusion.55
  12.4 0.1 copy.37
  12.5 6.3 %convert_bitcast_fusion = bf16[16,512,160]{1,2,0:T(8,128)(2,1)S(1)} fusion(bf16[16,512,512]{2,1,0:T(8,128)(2,1)} %param.11, bf16[512,128]{0,1:T(8,128)(2,1)S(1)} %bitcast.53, bf16[512,16]{0,1:T(8,128)(2,1)S(1)} %convolution_convert_fusion.2, bf16[512,16]{0,1:T(8,128)(2,1)S(1)} %convolution_convert_fusion.3), kind=kOutput, calls=%fused_computation | convolution fusion | flops 1343979520 | bytes 11173888 | tf_op jit(solution)/shard_map/esd,dc->esc/dot_general | solution.py:61
  18.8 0.0 copy-start.1
  18.8 0.1 copy.38
  18.9 7.1 %convert_bitcast_fusion.2 = bf16[16,512,144]{1,2,0:T(8,128)(2,1)S(1)} fusion(bf16[16,512,512]{2,1,0:T(8,128)(2,1)} %param.12, bf16[512,16]{0,1:T(8,128)(2,1)S(1)} %convolution_convert_fusion.1, bf16[512,128]{0,1:T(8,128)(2,1)S(1)} %bitcast.49), kind=kOutput, calls=%fused_computation.2 | convolution fusion | flops 1209434112 | bytes 10895360 | tf_op jit(solution)/shard_map/esd,dc->esc/dot_general | solution.py:61
  26.0 0.0 copy-done.1
  26.0 0.0 copy-start.3
  26.1 0.0 copy-start.8
  26.1 0.0 slice-start
  26.1 7.1 %convert_bitcast_fusion.1 = bf16[16,512,144]{1,2,0:T(8,128)(2,1)S(1)} fusion(bf16[16,512,512]{2,1,0:T(8,128)(2,1)} %param.13, bf16[512,16]{0,1:T(8,128)(2,1)S(1)} %convolution_convert_fusion, bf16[512,128]{0,1:T(8,128)(2,1)S(1)} %bitcast.50), kind=kOutput, calls=%fused_computation.1 | convolution fusion | flops 1209434112 | bytes 10895360 | tf_op jit(solution)/shard_map/esd,dc->esc/dot_general | solution.py:61
  33.2 0.0 copy-done.3
  33.2 0.0 copy-start.5
  33.2 0.0 copy-start.2
  33.2 1.4 copy-done.5
  34.6 0.0 copy-done.8
  34.6 0.1 iota_compare_fusion
  34.7 0.0 slice-done
  34.7 1.3 maximum_select_fusion
  36.0 0.0 all-reduce.4.cloned.1.call-update
  36.0 0.0 reduce-scatter.2.cloned.1.call-start
  36.1 59.4 %all-reduce.4.cloned.1.call-done = bf16[16,512,64]{1,2,0:T(8,128)(2,1)} async-done(((bf16[16,512,64]{1,2,0:T(8,128)(2,1)}), bf16[16,512,64]{1,2,0:T(8,128)(2,1)}) %all-reduce.4.cloned.1.call-update) | async-done | bytes 1048592 | tf_op jit(solution)/shard_map/psum | solution.py:71
  95.5 0.0 copy-done.2
  95.5 0.0 copy-start.4
  95.5 0.0 copy-start.9
  95.5 1.7 fusion.8
  97.2 0.0 copy-start.6
  97.2 1.8 fusion.11
  99.0 0.0 copy-done.4
  99.0 0.0 copy-done.9
  99.0 0.0 copy-start.7
  99.0 0.6 fusion.14
  99.7 0.0 copy-done.6
  99.7 0.7 fusion.17
  100.4 0.9 copy.42
  101.2 0.0 reduce-scatter.2.cloned.1.call-update
  101.3 0.0 all-reduce.6.cloned.1.call-start
  101.3 0.0 copy-done.7
  101.3 0.2 multiply_reduce_fusion
  101.5 0.7 dynamic-slice_multiply_fusion.1
  102.2 31.9 %reduce-scatter.2.cloned.1.call-done = bf16[16,1024]{1,0:T(8,128)(2,1)} async-done(((bf16[16,8192]{1,0:T(8,128)(2,1)}), bf16[16,1024]{1,0:T(8,128)(2,1)}) %reduce-scatter.2.cloned.1.call-update) | async-done | bytes 32784 | tf_op jit(solution)/shard_map/reduce_scatter | solution.py:90
  134.1 0.8 fusion.42
  134.9 13.5 %all_gather.3 = bf16[64,1024]{1,0:T(8,128)(2,1)S(1)} all-gather(bf16[16,1024]{1,0:T(8,128)(2,1)S(1)} %fusion.42), channel_id=1, replica_groups=mesh['tp'=8,'dp'=4] {'dp'}, dimensions={0}, use_global_device_ids=true | all-gather | bytes 163840 | tf_op jit(solution)/shard_map/all_gather | solution.py:97
  148.4 0.3 fusion.56
  148.7 0.1 multiply_reduce_fusion.1
  148.8 0.1 broadcast_in_dim.28
  148.9 0.7 pad_maximum_fusion.1
  149.6 0.0 all-reduce.6.cloned.1.call-update
  149.6 52.0 %all-reduce.6.cloned.1.call-done = f32[4,24,384]{2,1,0:T(8,128)} async-done(((f32[4,24,384]{2,1,0:T(8,128)}), f32[4,24,384]{2,1,0:T(8,128)}) %all-reduce.6.cloned.1.call-update) | async-done | bytes 147472 | tf_op jit(solution)/shard_map/psum | solution.py:110
  201.6 4.6 %all-to-all-start = ((f32[4,24,384]{2,1,0:T(8,128)}), f32[4,24,384]{2,1,0:T(8,128)S(1)}, u32[]{:S(2)}, u32[]{:S(2)}) async-start(f32[4,24,384]{2,1,0:T(8,128)} %all-reduce.6.cloned.1.call-done), calls=%async_computation.1 | async-start | bytes 294912 | tf_op jit(solution)/shard_map/all_to_all | solution.py:111
  206.2 6.6 %all-to-all-done = f32[4,24,384]{2,1,0:T(8,128)S(1)} async-done(((f32[4,24,384]{2,1,0:T(8,128)}), f32[4,24,384]{2,1,0:T(8,128)S(1)}, u32[]{:S(2)}, u32[]{:S(2)}) %all-to-all-start) | async-done | bytes 147488 | tf_op jit(solution)/shard_map/all_to_all | solution.py:111
  212.9 0.1 fusion.47
  213.0 0.7 fusion.49
  (9 shorter events, 0.1 us)
Async XLA Ops:
  6.5 0.7 copy-start
  6.5 88.9 %all-reduce.4.cloned.1.call-start = ((), (), s32[]{:S(2)}) async-start(), calls=%async_computation.2 | async-start | bytes 2097152 | tf_op jit(solution)/shard_map/psum | solution.py:71
  18.8 7.2 %copy-start.1 = (bf16[16,512,160]{1,2,0:T(8,128)(2,1)}, bf16[16,512,160]{1,2,0:T(8,128)(2,1)S(1)}, u32[]{:S(2)}) copy-start(bf16[16,512,160]{1,2,0:T(8,128)(2,1)S(1)} %convert_bitcast_fusion) | copy-start | bytes 7864324
  26.0 7.2 %copy-start.3 = (bf16[16,512,144]{1,2,0:T(8,128)(2,1)}, bf16[16,512,144]{1,2,0:T(8,128)(2,1)S(1)}, u32[]{:S(2)}) copy-start(bf16[16,512,144]{1,2,0:T(8,128)(2,1)S(1)} %convert_bitcast_fusion.2) | copy-start | bytes 7077892
  26.1 8.6 %copy-start.8 = (s32[16]{0:T(128)S(1)}, s32[16]{0:T(128)}, u32[]{:S(2)}) copy-start(s32[16]{0:T(128)} %param.14) | copy-start | bytes 196
  26.1 8.6 %slice-start = ((bf16[16,512,160]{1,2,0:T(8,128)(2,1)}), bf16[16,512,32]{1,2,0:T(8,128)(2,1)S(1)}, s32[]{:S(2)}) async-start(bf16[16,512,160]{1,2,0:T(8,128)(2,1)} %copy-done.1), calls=%async_computation.5 | async-start | bytes 1048576 | tf_op jit(solution)/shard_map/slice | solution.py:68
  33.2 1.4 copy-start.5
  33.2 62.3 %copy-start.2 = (bf16[16,512,160]{1,2,0:T(8,128)(2,1)S(1)}, bf16[16,512,160]{1,2,0:T(8,128)(2,1)}, u32[]{:S(2)}) copy-start(bf16[16,512,160]{1,2,0:T(8,128)(2,1)} %copy-done.1) | copy-start | bytes 7864324
  36.0 98.1 %reduce-scatter.2.cloned.1.call-start = ((), (), s32[]{:S(2)}) async-start(), calls=%async_computation.3 | async-start | bytes 294912 | tf_op jit(solution)/shard_map/reduce_scatter | solution.py:90
  95.5 3.5 %copy-start.4 = (bf16[16,512,144]{1,2,0:T(8,128)(2,1)S(1)}, bf16[16,512,144]{1,2,0:T(8,128)(2,1)}, u32[]{:S(2)}) copy-start(bf16[16,512,144]{1,2,0:T(8,128)(2,1)} %copy-done.3) | copy-start | bytes 7077892
  95.5 3.5 %copy-start.9 = (bf16[16,512,64]{1,2,0:T(8,128)(2,1)S(1)}, bf16[16,512,64]{1,2,0:T(8,128)(2,1)}, u32[]{:S(2)}) copy-start(bf16[16,512,64]{1,2,0:T(8,128)(2,1)} %all-reduce.4.cloned.1.call-done) | copy-start | bytes 3145732
  97.2 2.4 %copy-start.6 = (bf16[16,512,144]{1,2,0:T(8,128)(2,1)S(1)}, bf16[16,512,144]{1,2,0:T(8,128)(2,1)}, u32[]{:S(2)}) copy-start(bf16[16,512,144]{1,2,0:T(8,128)(2,1)} %copy-done.5) | copy-start | bytes 7077892
  99.0 2.3 %copy-start.7 = (bf16[256,1024]{1,0:T(8,128)(2,1)S(1)}, bf16[256,1024]{1,0:T(8,128)(2,1)}, u32[]{:S(2)}) copy-start(bf16[256,1024]{1,0:T(8,128)(2,1)} %param.21) | copy-start | bytes 1572868
  101.3 100.4 %all-reduce.6.cloned.1.call-start = ((), (), s32[]{:S(2)}) async-start(), calls=%async_computation.4 | async-start | bytes 294912 | tf_op jit(solution)/shard_map/psum | solution.py:110
  201.6 11.2 %all-to-all-start = ((f32[4,24,384]{2,1,0:T(8,128)}), f32[4,24,384]{2,1,0:T(8,128)S(1)}, u32[]{:S(2)}, u32[]{:S(2)}) async-start(f32[4,24,384]{2,1,0:T(8,128)} %all-reduce.6.cloned.1.call-done), calls=%async_computation.1 | async-start | bytes 294912 | tf_op jit(solution)/shard_map/all_to_all | solution.py:111
Sparse Core Ops, SparseCore 0:
  36.1 59.2 all-reduce.3
  101.4 32.6 reduce-scatter.1
  149.8 51.8 all-reduce.5
where the time goes:
time: 221 us; the launch traced here: 220 us
  waiting for transfers between devices  150 us (68%)
  matrix products  29.7 us (13%)
  blocking collectives  13.5 us (6%)
  between operations  13.3 us (6%)
  other arithmetic  4.71 us (2%)
  starting transfers between devices  4.69 us (2%)
  local copies, waits for them, and re-layouts  4.36 us (2%)
    psum x1, waiting for transfers between devices, body(): narrow = lax.psum(narrow, 'tp')  59.4 us
    psum x1, waiting for transfers between devices, body(): rows = lax.psum(rows, 'tp')  52 us
    reduce_scatter x1, waiting for transfers between devices, body(): lax.psum_scatter(own_features.astype(jnp.bfloat16), 'tp', scatter_dimensi...  31.9 us
    dot_general x3, matrix products, project(): jnp.einsum('esd,dc->esc', rows, weights, preferred_element_type=jnp.float32)  20.4 us
    all_gather x1, blocking collectives, body(): update = lax.all_gather(update, 'dp', axis=0, tiled=True)  13.5 us
    all_to_all x1, waiting for transfers between devices, body(): rows = lax.all_to_all(rows, 'dp', split_axis=0, concat_axis=0, tiled=True)  6.65 us
    dot_general x4, matrix products, outer_sum(): jnp.einsum('esr,esk->erk', narrow[..., first * rank_cols:(first + 1) * ra...  4.82 us
    all_to_all x1, starting transfers between devices, body(): rows = lax.all_to_all(rows, 'dp', split_axis=0, concat_axis=0, tiled=True)  4.6 us
  transfers between devices with their start and end apart: 4, of which 4 were waited for; matrix products, arithmetic and copies ran while one was open for 0% of the time, Pallas kernels for 0%

commit v1 on v0

--- a/solution.py
+++ b/solution.py
@@ -94,7 +94,12 @@
     first_moment = lax.dynamic_slice_in_dim(projected_first_moment, member * span, span)
     second_moment = lax.dynamic_slice_in_dim(projected_second_moment, member * span, span)
     update = adam_update(features, first_moment, second_moment).astype(jnp.bfloat16)
-    update = lax.all_gather(update, "dp", axis=0, tiled=True)
+    ring = [update]
+    for hop in range(3):
+        ring.append(lax.ppermute(ring[-1], "dp", [(dev, (dev + 1) % 4) for dev in range(4)]))
+    update = jnp.roll(
+        jnp.concatenate(ring[::-1], axis=0), (lax.axis_index("dp") + 1) * ring[0].shape[0], axis=0
+    )
     wide_update = update.astype(jnp.float32)
     target_float = targets.astype(jnp.float32)
     update_sq = jnp.sum(wide_update * wide_update, axis=1)

time: 221 us -> 224 us (1.014)
  blocking collectives: 13.5 us -> 0 us
  waiting for transfers between devices: 150 us -> 163 us
    ppermute x0 -> x3, waiting for transfers between devices: none -> 15.4 us  [body(): lax.ppermute(ring[-1], 'dp', [(dev, (dev + 1) % 4) for dev in range(4)])]
    all_gather x1 -> x0, blocking collectives: 13.5 us -> none  [body(): update = lax.all_gather(update, 'dp', axis=0, tiled=True)]
    psum x1, waiting for transfers between devices: 52 us -> 49.3 us  [body(): rows = lax.psum(rows, 'tp')]
  transfers between devices with their start and end apart: 4 -> 7, of which waited for: 4 -> 7; matrix products, arithmetic and copies ran while one was open for 0% -> 0% of each run, Pallas kernels for 0% -> 0%
where the time goes in v1:
time: 224 us; the launch traced here: 223 us
  waiting for transfers between devices  163 us (73%)
  matrix products  29.7 us (13%)
  between operations  13.4 us (6%)
  other arithmetic  6.34 us (3%)
  starting transfers between devices  6.22 us (3%)
  local copies, waits for them, and re-layouts  4.39 us (2%)
    psum x1, waiting for transfers between devices, body(): narrow = lax.psum(narrow, 'tp')  59.4 us
    psum x1, waiting for transfers between devices, body(): rows = lax.psum(rows, 'tp')  49.3 us
    reduce_scatter x1, waiting for transfers between devices, body(): lax.psum_scatter(own_features.astype(jnp.bfloat16), 'tp', scatter_dimensi...  32.1 us
    dot_general x3, matrix products, project(): jnp.einsum('esd,dc->esc', rows, weights, preferred_element_type=jnp.float32)  20.4 us
    ppermute x3, waiting for transfers between devices, body(): lax.ppermute(ring[-1], 'dp', [(dev, (dev + 1) % 4) for dev in range(4)])  15.4 us
    all_to_all x1, waiting for transfers between devices, body(): rows = lax.all_to_all(rows, 'dp', split_axis=0, concat_axis=0, tiled=True)  6.65 us
    dot_general x4, matrix products, outer_sum(): jnp.einsum('esr,esk->erk', narrow[..., first * rank_cols:(first + 1) * ra...  4.82 us
    all_to_all x1, starting transfers between devices, body(): rows = lax.all_to_all(rows, 'dp', split_axis=0, concat_axis=0, tiled=True)  4.6 us
  transfers between devices with their start and end apart: 7, of which 7 were waited for; matrix products, arithmetic and copies ran while one was open for 0% of the time, Pallas kernels for 0%

profile of v1, /device:TPU:0, one launch (start us, length us, event | category | flops | bytes accessed | tf_op | source)
XLA Modules:
  0.0 222.9 jit_solution(7167127876675321850)
XLA Ops:
  6.5 0.0 copy-start
  6.5 0.0 all-reduce.4.cloned.1.call-start
  6.5 0.7 copy-done
  7.2 1.0 convolution_convert_fusion.2
  8.3 1.1 convolution_convert_fusion.3
  9.3 1.0 convolution_convert_fusion.1
  10.4 1.0 convolution_convert_fusion
  11.4 1.0 fusion.58
  12.4 0.1 copy.37
  12.5 6.3 %convert_bitcast_fusion = bf16[16,512,160]{1,2,0:T(8,128)(2,1)S(1)} fusion(bf16[16,512,512]{2,1,0:T(8,128)(2,1)} %param.11, bf16[512,128]{0,1:T(8,128)(2,1)S(1)} %bitcast.52, bf16[512,16]{0,1:T(8,128)(2,1)S(1)} %convolution_convert_fusion.2, bf16[512,16]{0,1:T(8,128)(2,1)S(1)} %convolution_convert_fusion.3), kind=kOutput, calls=%fused_computation | convolution fusion | flops 1343979520 | bytes 11173888 | tf_op jit(solution)/shard_map/esd,dc->esc/dot_general | solution.py:61
  18.8 0.0 copy-start.1
  18.8 0.1 copy.38
  18.9 7.1 %convert_bitcast_fusion.2 = bf16[16,512,144]{1,2,0:T(8,128)(2,1)S(1)} fusion(bf16[16,512,512]{2,1,0:T(8,128)(2,1)} %param.12, bf16[512,16]{0,1:T(8,128)(2,1)S(1)} %convolution_convert_fusion.1, bf16[512,128]{0,1:T(8,128)(2,1)S(1)} %bitcast.48), kind=kOutput, calls=%fused_computation.2 | convolution fusion | flops 1209434112 | bytes 10895360 | tf_op jit(solution)/shard_map/esd,dc->esc/dot_general | solution.py:61
  26.0 0.0 copy-done.1
  26.0 0.0 copy-start.3
  26.1 0.0 copy-start.8
  26.1 0.0 slice-start
  26.1 7.1 %convert_bitcast_fusion.1 = bf16[16,512,144]{1,2,0:T(8,128)(2,1)S(1)} fusion(bf16[16,512,512]{2,1,0:T(8,128)(2,1)} %param.13, bf16[512,16]{0,1:T(8,128)(2,1)S(1)} %convolution_convert_fusion, bf16[512,128]{0,1:T(8,128)(2,1)S(1)} %bitcast.49), kind=kOutput, calls=%fused_computation.1 | convolution fusion | flops 1209434112 | bytes 10895360 | tf_op jit(solution)/shard_map/esd,dc->esc/dot_general | solution.py:61
  33.2 0.0 copy-done.3
  33.2 0.0 copy-start.5
  33.2 0.0 copy-start.2
  33.2 1.4 copy-done.5
  34.6 0.0 copy-done.8
  34.6 0.1 iota_compare_fusion
  34.7 0.0 slice-done
  34.7 1.3 maximum_select_fusion
  36.0 0.0 all-reduce.4.cloned.1.call-update
  36.0 0.0 reduce-scatter.2.cloned.1.call-start
  36.1 59.4 %all-reduce.4.cloned.1.call-done = bf16[16,512,64]{1,2,0:T(8,128)(2,1)} async-done(((bf16[16,512,64]{1,2,0:T(8,128)(2,1)}), bf16[16,512,64]{1,2,0:T(8,128)(2,1)}) %all-reduce.4.cloned.1.call-update) | async-done | bytes 1048592 | tf_op jit(solution)/shard_map/psum | solution.py:71
  95.5 0.0 copy-done.2
  95.5 1.7 fusion.8
  97.2 1.8 fusion.11
  99.0 0.0 copy-done.4
  99.0 0.0 copy-done.9
  99.0 0.0 copy-start.7
  99.0 0.6 fusion.14
  99.7 0.0 copy-done.6
  99.7 0.7 fusion.17
  100.4 0.9 copy.42
  101.3 0.0 reduce-scatter.2.cloned.1.call-update
  101.3 0.0 all-reduce.6.cloned.1.call-start
  101.4 0.7 dynamic-slice_multiply_fusion.1
  102.1 32.1 %reduce-scatter.2.cloned.1.call-done = bf16[16,1024]{1,0:T(8,128)(2,1)} async-done(((bf16[16,8192]{1,0:T(8,128)(2,1)}), bf16[16,1024]{1,0:T(8,128)(2,1)}) %reduce-scatter.2.cloned.1.call-update) | async-done | bytes 32784 | tf_op jit(solution)/shard_map/reduce_scatter | solution.py:90
  134.2 0.8 fusion.44
  135.0 1.5 collective-permute-start
  136.5 4.2 %collective-permute-done = bf16[16,1024]{1,0:T(8,128)(2,1)S(1)} collective-permute-done((bf16[16,1024]{1,0:T(8,128)(2,1)S(1)}, bf16[16,1024]{1,0:T(8,128)(2,1)S(1)}, u32[]{:S(2)}, u32[]{:S(2)}) %collective-permute-start) | collective-permute-done | bytes 32800 | tf_op jit(solution)/shard_map/ppermute | solution.py:99
  140.7 0.0 collective-permute-start.1
  140.7 5.7 %collective-permute-done.1 = bf16[16,1024]{1,0:T(8,128)(2,1)S(1)} collective-permute-done((bf16[16,1024]{1,0:T(8,128)(2,1)S(1)}, bf16[16,1024]{1,0:T(8,128)(2,1)S(1)}, u32[]{:S(2)}, u32[]{:S(2)}) %collective-permute-start.1) | collective-permute-done | bytes 32800 | tf_op jit(solution)/shard_map/ppermute | solution.py:99
  146.4 0.0 collective-permute-start.2
  146.4 0.0 copy-done.7
  146.5 0.2 multiply_reduce_fusion
  146.7 5.5 %collective-permute-done.2 = bf16[16,1024]{1,0:T(8,128)(2,1)S(1)} collective-permute-done((bf16[16,1024]{1,0:T(8,128)(2,1)S(1)}, bf16[16,1024]{1,0:T(8,128)(2,1)S(1)}, u32[]{:S(2)}, u32[]{:S(2)}) %collective-permute-start.2) | collective-permute-done | bytes 32800 | tf_op jit(solution)/shard_map/ppermute | solution.py:99
  152.2 0.8 constant_dynamic-update-slice_fusion.4
  153.0 0.8 constant_dynamic-update-slice_fusion
  153.8 0.3 fusion.40
  154.1 0.1 multiply_reduce_fusion.1
  154.2 0.1 broadcast_in_dim.28
  154.4 0.7 pad_maximum_fusion.1
  155.0 0.0 all-reduce.6.cloned.1.call-update
  155.0 49.3 %all-reduce.6.cloned.1.call-done = f32[4,24,384]{2,1,0:T(8,128)} async-done(((f32[4,24,384]{2,1,0:T(8,128)}), f32[4,24,384]{2,1,0:T(8,128)}) %all-reduce.6.cloned.1.call-update) | async-done | bytes 147472 | tf_op jit(solution)/shard_map/psum | solution.py:115
  204.3 4.6 %all-to-all-start = ((f32[4,24,384]{2,1,0:T(8,128)}), f32[4,24,384]{2,1,0:T(8,128)S(1)}, u32[]{:S(2)}, u32[]{:S(2)}) async-start(f32[4,24,384]{2,1,0:T(8,128)} %all-reduce.6.cloned.1.call-done), calls=%async_computation.1 | async-start | bytes 294912 | tf_op jit(solution)/shard_map/all_to_all | solution.py:116
  208.9 6.6 %all-to-all-done = f32[4,24,384]{2,1,0:T(8,128)S(1)} async-done(((f32[4,24,384]{2,1,0:T(8,128)}), f32[4,24,384]{2,1,0:T(8,128)S(1)}, u32[]{:S(2)}, u32[]{:S(2)}) %all-to-all-start) | async-done | bytes 147488 | tf_op jit(solution)/shard_map/all_to_all | solution.py:116
  215.6 0.1 fusion.49
  215.7 0.7 fusion.51
  (18 shorter events, 0.2 us)
Async XLA Ops:
  6.5 0.7 copy-start
  6.5 89.0 %all-reduce.4.cloned.1.call-start = ((), (), s32[]{:S(2)}) async-start(), calls=%async_computation.2 | async-start | bytes 2097152 | tf_op jit(solution)/shard_map/psum | solution.py:71
  18.8 7.2 %copy-start.1 = (bf16[16,512,160]{1,2,0:T(8,128)(2,1)}, bf16[16,512,160]{1,2,0:T(8,128)(2,1)S(1)}, u32[]{:S(2)}) copy-start(bf16[16,512,160]{1,2,0:T(8,128)(2,1)S(1)} %convert_bitcast_fusion) | copy-start | bytes 7864324
  26.0 7.2 %copy-start.3 = (bf16[16,512,144]{1,2,0:T(8,128)(2,1)}, bf16[16,512,144]{1,2,0:T(8,128)(2,1)S(1)}, u32[]{:S(2)}) copy-start(bf16[16,512,144]{1,2,0:T(8,128)(2,1)S(1)} %convert_bitcast_fusion.2) | copy-start | bytes 7077892
  26.1 8.6 %copy-start.8 = (s32[16]{0:T(128)S(1)}, s32[16]{0:T(128)}, u32[]{:S(2)}) copy-start(s32[16]{0:T(128)} %param.14) | copy-start | bytes 196
  26.1 8.6 %slice-start = ((bf16[16,512,160]{1,2,0:T(8,128)(2,1)}), bf16[16,512,32]{1,2,0:T(8,128)(2,1)S(1)}, s32[]{:S(2)}) async-start(bf16[16,512,160]{1,2,0:T(8,128)(2,1)} %copy-done.1), calls=%async_computation.5 | async-start | bytes 1048576 | tf_op jit(solution)/shard_map/slice | solution.py:68
  33.2 1.4 copy-start.5
  33.2 62.3 %copy-start.2 = (bf16[16,512,160]{1,2,0:T(8,128)(2,1)S(1)}, bf16[16,512,160]{1,2,0:T(8,128)(2,1)}, u32[]{:S(2)}) copy-start(bf16[16,512,160]{1,2,0:T(8,128)(2,1)} %copy-done.1) | copy-start | bytes 7864324
  36.0 98.1 %reduce-scatter.2.cloned.1.call-start = ((), (), s32[]{:S(2)}) async-start(), calls=%async_computation.3 | async-start | bytes 294912 | tf_op jit(solution)/shard_map/reduce_scatter | solution.py:90
  95.5 3.5 %copy-start.4 = (bf16[16,512,144]{1,2,0:T(8,128)(2,1)S(1)}, bf16[16,512,144]{1,2,0:T(8,128)(2,1)}, u32[]{:S(2)}) copy-start(bf16[16,512,144]{1,2,0:T(8,128)(2,1)} %copy-done.3) | copy-start | bytes 7077892
  95.5 3.5 %copy-start.9 = (bf16[16,512,64]{1,2,0:T(8,128)(2,1)S(1)}, bf16[16,512,64]{1,2,0:T(8,128)(2,1)}, u32[]{:S(2)}) copy-start(bf16[16,512,64]{1,2,0:T(8,128)(2,1)} %all-reduce.4.cloned.1.call-done) | copy-start | bytes 3145732
  97.2 2.4 %copy-start.6 = (bf16[16,512,144]{1,2,0:T(8,128)(2,1)S(1)}, bf16[16,512,144]{1,2,0:T(8,128)(2,1)}, u32[]{:S(2)}) copy-start(bf16[16,512,144]{1,2,0:T(8,128)(2,1)} %copy-done.5) | copy-start | bytes 7077892
  99.0 47.4 %copy-start.7 = (bf16[256,1024]{1,0:T(8,128)(2,1)S(1)}, bf16[256,1024]{1,0:T(8,128)(2,1)}, u32[]{:S(2)}) copy-start(bf16[256,1024]{1,0:T(8,128)(2,1)} %param.21) | copy-start | bytes 1572868
  101.3 103.0 %all-reduce.6.cloned.1.call-start = ((), (), s32[]{:S(2)}) async-start(), calls=%async_computation.4 | async-start | bytes 294912 | tf_op jit(solution)/shard_map/psum | solution.py:115
  135.0 5.8 %collective-permute-start = (bf16[16,1024]{1,0:T(8,128)(2,1)S(1)}, bf16[16,1024]{1,0:T(8,128)(2,1)S(1)}, u32[]{:S(2)}, u32[]{:S(2)}) collective-permute-start(bf16[16,1024]{1,0:T(8,128)(2,1)S(1)} %fusion.44), channel_id=1, source_target_pairs={{0,1},{1,2},{2,3},{3,0},{4,5},{5,6},{6,7},{7,4},{8,9},{9,10},{10,1... | collective-permute-start | bytes 98312 | tf_op jit(solution)/shard_map/ppermute | solution.py:99
  140.7 5.7 %collective-permute-start.1 = (bf16[16,1024]{1,0:T(8,128)(2,1)S(1)}, bf16[16,1024]{1,0:T(8,128)(2,1)S(1)}, u32[]{:S(2)}, u32[]{:S(2)}) collective-permute-start(bf16[16,1024]{1,0:T(8,128)(2,1)S(1)} %collective-permute-done), channel_id=1, source_target_pairs={{0,1},{1,2},{2,3},{3,0},{4,5},{5,6},{6,7},{7,4},{8,9},{9,10},{10,1... | collective-permute-start | bytes 98312 | tf_op jit(solution)/shard_map/ppermute | solution.py:99
  146.4 5.7 %collective-permute-start.2 = (bf16[16,1024]{1,0:T(8,128)(2,1)S(1)}, bf16[16,1024]{1,0:T(8,128)(2,1)S(1)}, u32[]{:S(2)}, u32[]{:S(2)}) collective-permute-start(bf16[16,1024]{1,0:T(8,128)(2,1)S(1)} %collective-permute-done.1), channel_id=1, source_target_pairs={{0,1},{1,2},{2,3},{3,0},{4,5},{5,6},{6,7},{7,4},{8,9},{9,10},{10,1... | collective-permute-start | bytes 98312 | tf_op jit(solution)/shard_map/ppermute | solution.py:99
  204.3 11.2 %all-to-all-start = ((f32[4,24,384]{2,1,0:T(8,128)}), f32[4,24,384]{2,1,0:T(8,128)S(1)}, u32[]{:S(2)}, u32[]{:S(2)}) async-start(f32[4,24,384]{2,1,0:T(8,128)} %all-reduce.6.cloned.1.call-done), calls=%async_computation.1 | async-start | bytes 294912 | tf_op jit(solution)/shard_map/all_to_all | solution.py:116
Sparse Core Ops, SparseCore 0:
  36.2 59.2 all-reduce.3
  101.4 32.6 reduce-scatter.1
  155.2 49.1 all-reduce.5
